TPU v7x, 32 devices: a whole 2x2x4 slice. The times are simulated.
32 devices in a mesh: batch: 8 (over y, x, core), rows: 4 (over z).
Axes of the slice: x: 2, y: 2, z: 4, core: 2. Of those that a mesh axis runs over, the one named last changes fastest.
Arguments:
- fine_level: bfloat16 [8, 32, 192, 384], P('batch', 'rows'), may hold values from -40 to 40
- middle_level: bfloat16 [8, 16, 96, 384], P('batch', 'rows'), may hold values from -40 to 40
- coarse_level: bfloat16 [8, 8, 48, 384], P('batch', 'rows'), may hold values from -40 to 40
- two_input_weights: float32 [2, 3, 2], replicated, may hold values from 0.5 to 2
- three_input_weights: float32 [2, 3], replicated, may hold values from 0.5 to 2
- depthwise: bfloat16 [2, 4, 3, 3, 384], replicated, may hold values from -2 to 2
- pointwise: bfloat16 [2, 4, 384, 384], replicated, may hold values from -0.3125 to 0.3125
- bn_gain: float32 [2, 4, 384], replicated, may hold values from 0.5 to 1.5
- bn_bias: float32 [2, 4, 384], replicated, may hold values from -3 to 3
Outputs:
- fine_result: bfloat16 [8, 32, 192, 384], P('batch', 'rows')
- middle_result: bfloat16 [8, 16, 96, 384], P('batch', 'rows')
- coarse_result: bfloat16 [8, 8, 48, 384], P('batch', 'rows')
All inputs are finite; a program needn't handle non-finite values.
Results may differ from a plain program's by a relative error of at most 0.025.
Values may be sent and summed in bfloat16 or wider, within the bound.
A program may use at most 64 MiB of HBM per device.

v0:
```python
import jax
import jax.numpy as jnp
from jax import lax
from jax.sharding import PartitionSpec as P

LAYERS = 2


def from_behind(block, axis, distance):
    devices = range(lax.axis_size(axis))
    route = [(i - distance, i) for i in devices if i - distance in devices]
    return lax.ppermute(block, axis, route)


def extended_2(block, sides, width):
    for axis, dim in sides:
        count = lax.axis_size(axis)
        forward = [(i, i + 1) for i in range(count - 1)]
        backward = [(target, source) for source, target in forward]
        low = lax.ppermute(
            lax.slice_in_dim(block, block.shape[dim] - width, None, axis=dim), axis, forward
        )
        high = lax.ppermute(lax.slice_in_dim(block, 0, width, axis=dim), axis, backward)
        block = jnp.concatenate([low, block, high], axis=dim)
    return block


def upsample(feature_maps):
    return jnp.repeat(jnp.repeat(feature_maps, 2, axis=1), 2, axis=2)


def reduce_resolution(feature_maps):
    beneath = from_behind(feature_maps[:, :1], "rows", -1)
    lowest = jnp.array(-jnp.inf, feature_maps.dtype)
    at_bottom = lax.axis_index("rows") == lax.axis_size("rows") - 1
    beneath = jnp.where(at_bottom, lowest, beneath)
    extended = jnp.concatenate([feature_maps, beneath], axis=1)
    padded = jnp.pad(extended, ((0, 0), (0, 0), (0, 1), (0, 0)), constant_values=lowest)
    return lax.reduce_window(padded, lowest, lax.max, (1, 3, 3, 1), (1, 2, 2, 1), "VALID")


def weighted_join_activate(inputs_list, weights):
    weight_sum = jnp.sum(weights) + 0.0001
    running = weights[0] * inputs_list[0].astype(jnp.float32)
    for position in range(1, len(inputs_list)):
        running = running + weights[position] * inputs_list[position].astype(jnp.float32)
    return jax.nn.silu(running / weight_sum).astype(jnp.bfloat16)


def separable(extended, kernel, projection):
    padded = jnp.pad(extended, ((0, 0), (0, 0), (1, 1), (0, 0)))
    height = extended.shape[1] - 2
    width = extended.shape[2]
    running = jnp.zeros((extended.shape[0], height, width, extended.shape[3]), jnp.float32)
    for row_tap in range(3):
        for col_tap in range(3):
            window = padded[:, row_tap : row_tap + height, col_tap : col_tap + width, :]
            running = running + window.astype(jnp.float32) * kernel[row_tap, col_tap].astype(
                jnp.float32
            )
    spatial = running.astype(jnp.bfloat16)
    projected = jnp.dot(
        spatial.reshape(-1, spatial.shape[-1]), projection, preferred_element_type=jnp.float32
    )
    return projected.reshape(spatial.shape)


def normalize(projected, gain, offset):
    count = float(
        projected.shape[0]
        * projected.shape[1]
        * projected.shape[2]
        * lax.axis_size("batch")
        * lax.axis_size("rows")
    )
    totals, squares = lax.psum(
        (jnp.sum(projected, axis=(0, 1, 2)), jnp.sum(projected * projected, axis=(0, 1, 2))),
        ("batch", "rows"),
    )
    center = totals / count
    spread = squares / count - center * center
    centered = projected - center
    return (centered * lax.rsqrt(spread + 1e-05) * gain + offset).astype(jnp.bfloat16)


def node(activated, kernel, projection, gain, offset):
    extended = extended_2(activated, (("rows", 1),), 1)
    return normalize(separable(extended, kernel, projection), gain, offset)


def body(
    fine_level,
    middle_level,
    coarse_level,
    two_input_weights,
    three_input_weights,
    depthwise,
    pointwise,
    bn_gain,
    bn_bias,
):
    fine, middle_grid, coarse_grid = (fine_level, middle_level, coarse_level)
    for bidirectional_layer in range(LAYERS):

        def run_layer_pair(index, activated):
            return node(
                activated,
                depthwise[bidirectional_layer, index],
                pointwise[bidirectional_layer, index],
                bn_gain[bidirectional_layer, index],
                bn_bias[bidirectional_layer, index],
            )

        downward_middle = run_layer_pair(
            0,
            weighted_join_activate(
                [middle_grid, upsample(coarse_grid)], two_input_weights[bidirectional_layer, 0]
            ),
        )
        updated_fine = run_layer_pair(
            1,
            weighted_join_activate(
                [fine, upsample(downward_middle)], two_input_weights[bidirectional_layer, 1]
            ),
        )
        updated_middle = run_layer_pair(
            2,
            weighted_join_activate(
                [middle_grid, downward_middle, reduce_resolution(updated_fine)],
                three_input_weights[bidirectional_layer],
            ),
        )
        updated_coarse = run_layer_pair(
            3,
            weighted_join_activate(
                [coarse_grid, reduce_resolution(updated_middle)],
                two_input_weights[bidirectional_layer, 2],
            ),
        )
        fine, middle_grid, coarse_grid = (updated_fine, updated_middle, updated_coarse)
    return (fine, middle_grid, coarse_grid)


def solution(mesh):
    in_specs = (
        P("batch", "rows", None, None),
        P("batch", "rows", None, None),
        P("batch", "rows", None, None),
        P(),
        P(),
        P(),
        P(),
        P(),
        P(),
    )
    out_specs = (
        P("batch", "rows", None, None),
        P("batch", "rows", None, None),
        P("batch", "rows", None, None),
    )
    return jax.shard_map(body, mesh=mesh, in_specs=in_specs, out_specs=out_specs, check_vma=False)
```

profile of v0, /device:TPU:0, one launch (start us, length us, event | category | flops | bytes accessed | tf_op | source)
XLA Modules:
  0.0 496.3 jit_solution(17493123043353743994)
XLA Ops:
  7.4 5.0 collective-permute-start
  20.6 40.4 %all-reduce.15 = (f32[384]{0:T(512)S(1)}, f32[384]{0:T(512)S(1)}) all-reduce(f32[384]{0:T(512)S(1)} %get-tuple-element.14, f32[384]{0:T(512)S(1)} %get-tuple-element.13), channel_id=1, replica_groups=mesh['batch'=8,'rows'=4] {'batch','rows'}, use_global_device_ids=true, to_apply=%region_4.5 | all-reduce | flops 768 | bytes 6144 | tf_op jit(solution)/shard_map/psum | solution.py:76
  74.4 4.4 collective-permute-done.3
  83.5 40.1 %all-reduce.14 = (f32[384]{0:T(512)S(1)}, f32[384]{0:T(512)S(1)}) all-reduce(f32[384]{0:T(512)S(1)} %get-tuple-element.6, f32[384]{0:T(512)S(1)} %get-tuple-element.5), channel_id=1, replica_groups=mesh['batch'=8,'rows'=4] {'batch','rows'}, use_global_device_ids=true, to_apply=%region_9.10 | all-reduce | flops 768 | bytes 6144 | tf_op jit(solution)/shard_map/psum | solution.py:76
  137.6 3.4 multiply_convert_fusion.4
  145.4 4.3 collective-permute-done.6
  151.8 40.2 %all-reduce.13 = (f32[384]{0:T(512)S(1)}, f32[384]{0:T(512)S(1)}) all-reduce(f32[384]{0:T(512)S(1)} %get-tuple-element.12, f32[384]{0:T(512)S(1)} %get-tuple-element.11), channel_id=1, replica_groups=mesh['batch'=8,'rows'=4] {'batch','rows'}, use_global_device_ids=true, to_apply=%region_15.16 | all-reduce | flops 768 | bytes 6144 | tf_op jit(solution)/shard_map/psum | solution.py:76
  194.7 3.7 collective-permute-done.7
  212.1 39.2 %all-reduce.12 = (f32[384]{0:T(512)S(1)}, f32[384]{0:T(512)S(1)}) all-reduce(f32[384]{0:T(512)S(1)} %get-tuple-element.18, f32[384]{0:T(512)S(1)} %get-tuple-element.17), channel_id=1, replica_groups=mesh['batch'=8,'rows'=4] {'batch','rows'}, use_global_device_ids=true, to_apply=%region_21.22 | all-reduce | flops 768 | bytes 6144 | tf_op jit(solution)/shard_map/psum | solution.py:76
  261.4 4.3 collective-permute-done.11
  267.7 40.0 %all-reduce.11 = (f32[384]{0:T(512)S(1)}, f32[384]{0:T(512)S(1)}) all-reduce(f32[384]{0:T(512)S(1)} %get-tuple-element.10, f32[384]{0:T(512)S(1)} %get-tuple-element.9), channel_id=1, replica_groups=mesh['batch'=8,'rows'=4] {'batch','rows'}, use_global_device_ids=true, to_apply=%region_26.27 | all-reduce | flops 768 | bytes 6144 | tf_op jit(solution)/shard_map/psum | solution.py:76
  311.3 4.1 mul.1555
  315.4 3.3 multiply_convert_fusion
  318.7 3.3 collective-permute-start.12
  324.7 4.4 collective-permute-done.13
  333.8 39.1 %all-reduce.10 = (f32[384]{0:T(512)S(1)}, f32[384]{0:T(512)S(1)}) all-reduce(f32[384]{0:T(512)S(1)} %get-tuple-element.4, f32[384]{0:T(512)S(1)} %get-tuple-element.3), channel_id=1, replica_groups=mesh['batch'=8,'rows'=4] {'batch','rows'}, use_global_device_ids=true, to_apply=%region_31.32 | all-reduce | flops 768 | bytes 6144 | tf_op jit(solution)/shard_map/psum | solution.py:76
  376.3 5.0 %collective-permute-done.14 = bf16[1,1,192,384]{3,2,1,0:T(8,128)(2,1)S(1)} collective-permute-done((bf16[1,1,192,384]{3,2,1,0:T(8,128)(2,1)S(1)}, bf16[1,1,192,384]{3,2,1,0:T(8,128)(2,1)S(1)}, u32[]{:S(2)}, u32[]{:S(2)}) %collective-permute-start.14) | collective-permute-done | bytes 147488 | tf_op jit(solution)/shard_map/ppermute | solution.py:12
  382.8 3.4 multiply_convert_fusion.2
  391.5 4.3 collective-permute-done.16
  397.8 40.1 %all-reduce.9 = (f32[384]{0:T(512)S(1)}, f32[384]{0:T(512)S(1)}) all-reduce(f32[384]{0:T(512)S(1)} %get-tuple-element.8, f32[384]{0:T(512)S(1)} %get-tuple-element.7), channel_id=1, replica_groups=mesh['batch'=8,'rows'=4] {'batch','rows'}, use_global_device_ids=true, to_apply=%region_37.38 | all-reduce | flops 768 | bytes 6144 | tf_op jit(solution)/shard_map/psum | solution.py:76
  440.1 4.3 collective-permute-done.17
  446.0 3.3 collective-permute-start.18
  451.0 4.2 collective-permute-done.19
  456.6 39.0 %all-reduce.8 = (f32[384]{0:T(512)S(1)}, f32[384]{0:T(512)S(1)}) all-reduce(f32[384]{0:T(512)S(1)} %get-tuple-element.16, f32[384]{0:T(512)S(1)} %get-tuple-element.15), channel_id=1, replica_groups=mesh['batch'=8,'rows'=4] {'batch','rows'}, use_global_device_ids=true, to_apply=%region_43.44 | all-reduce | flops 768 | bytes 6144 | tf_op jit(solution)/shard_map/psum | solution.py:76
  (243 shorter events, 106.4 us)
Async XLA Ops:
  7.4 9.0 %collective-permute-start = (bf16[1,1,96,384]{3,2,1,0:T(8,128)(2,1)S(1)}, bf16[1,1,96,384]{3,2,1,0:T(8,128)(2,1)S(1)}, u32[]{:S(2)}, u32[]{:S(2)}) collective-permute-start(bf16[1,1,96,384]{3,2,1,0:T(8,128)(2,1)S(1)} %get-tuple-element.141), channel_id=1, source_target_pairs={{0,1},{1,2},{2,3},{4,5},{5,6},{6,7},{8,9},{9,10},{10,11},{12,13},{... | collective-permute-start | bytes 221192 | tf_op jit(solution)/shard_map/ppermute | solution.py:20
  12.4 6.2 %collective-permute-start.1 = (bf16[1,1,96,384]{3,2,1,0:T(8,128)(2,1)S(1)}, bf16[1,1,96,384]{3,2,1,0:T(8,128)(2,1)S(1)}, u32[]{:S(2)}, u32[]{:S(2)}) collective-permute-start(bf16[1,1,96,384]{3,2,1,0:T(8,128)(2,1)S(1)} %get-tuple-element.142), channel_id=1, source_target_pairs={{1,0},{2,1},{3,2},{5,4},{6,5},{7,6},{9,8},{10,9},{11,10},{13,12},{... | collective-permute-start | bytes 221192 | tf_op jit(solution)/shard_map/ppermute | solution.py:23
  16.4 238.2 %copy-start.21 = (f32[384]{0:T(512)}, f32[384]{0:T(512)S(1)}, u32[]{:S(2)}) copy-start(f32[384]{0:T(512)S(1)} %get-tuple-element.31) | copy-start | bytes 4612
  69.4 5.0 %collective-permute-start.2 = (bf16[1,1,192,384]{3,2,1,0:T(8,128)(2,1)S(1)}, bf16[1,1,192,384]{3,2,1,0:T(8,128)(2,1)S(1)}, u32[]{:S(2)}, u32[]{:S(2)}) collective-permute-start(bf16[1,1,192,384]{3,2,1,0:T(8,128)(2,1)S(1)} %get-tuple-element.133), channel_id=1, source_target_pairs={{0,1},{1,2},{2,3},{4,5},{5,6},{6,7},{8,9},{9,10},{10,11},{12,13},{... | collective-permute-start | bytes 442376 | tf_op jit(solution)/shard_map/ppermute | solution.py:20
  71.7 7.0 %collective-permute-start.3 = (bf16[1,1,192,384]{3,2,1,0:T(8,128)(2,1)S(1)}, bf16[1,1,192,384]{3,2,1,0:T(8,128)(2,1)S(1)}, u32[]{:S(2)}, u32[]{:S(2)}) collective-permute-start(bf16[1,1,192,384]{3,2,1,0:T(8,128)(2,1)S(1)} %get-tuple-element.134), channel_id=1, source_target_pairs={{1,0},{2,1},{3,2},{5,4},{6,5},{7,6},{9,8},{10,9},{11,10},{13,12},{... | collective-permute-start | bytes 442376 | tf_op jit(solution)/shard_map/ppermute | solution.py:23
  125.9 7.3 %collective-permute-start.4 = (bf16[1,1,192,384]{3,2,1,0:T(8,128)(2,1)}, bf16[1,1,192,384]{3,2,1,0:T(8,128)(2,1)}, u32[]{:S(2)}, u32[]{:S(2)}) collective-permute-start(bf16[1,1,192,384]{3,2,1,0:T(8,128)(2,1)} %slice.974), channel_id=1, source_target_pairs={{1,0},{2,1},{3,2},{5,4},{6,5},{7,6},{9,8},{10,9},{11,10},{13,12},{... | collective-permute-start | bytes 442376 | tf_op jit(solution)/shard_map/ppermute | solution.py:12
  141.0 4.4 collective-permute-start.5
  143.5 6.2 %collective-permute-start.6 = (bf16[1,1,96,384]{3,2,1,0:T(8,128)(2,1)S(1)}, bf16[1,1,96,384]{3,2,1,0:T(8,128)(2,1)S(1)}, u32[]{:S(2)}, u32[]{:S(2)}) collective-permute-start(bf16[1,1,96,384]{3,2,1,0:T(8,128)(2,1)S(1)} %get-tuple-element.140), channel_id=1, source_target_pairs={{1,0},{2,1},{3,2},{5,4},{6,5},{7,6},{9,8},{10,9},{11,10},{13,12},{... | collective-permute-start | bytes 221192 | tf_op jit(solution)/shard_map/ppermute | solution.py:23
  151.7 102.8 %copy-start.1 = (f32[384,384]{1,0:T(8,128)}, f32[384,384]{1,0:T(8,128)S(1)}, u32[]{:S(2)}) copy-start(f32[384,384]{1,0:T(8,128)S(1)} %get-tuple-element.191) | copy-start | bytes 1769476
  151.7 99.6 %copy-start.32 = (f32[384]{0:T(512)S(1)}, f32[384]{0:T(512)}, u32[]{:S(2)}) copy-start(f32[384]{0:T(512)} %get-tuple-element.30) | copy-start | bytes 4612
  151.8 99.6 %copy-start.34 = (f32[384]{0:T(512)S(1)}, f32[384]{0:T(512)}, u32[]{:S(2)}) copy-start(f32[384]{0:T(512)} %get-tuple-element.209) | copy-start | bytes 4612
  192.1 6.2 %collective-permute-start.7 = (bf16[1,1,96,384]{3,2,1,0:T(8,128)(2,1)S(1)}, bf16[1,1,96,384]{3,2,1,0:T(8,128)(2,1)S(1)}, u32[]{:S(2)}, u32[]{:S(2)}) collective-permute-start(bf16[1,1,96,384]{3,2,1,0:T(8,128)(2,1)S(1)} %slice.992), channel_id=1, source_target_pairs={{1,0},{2,1},{3,2},{5,4},{6,5},{7,6},{9,8},{10,9},{11,10},{13,12},{... | collective-permute-start | bytes 221192 | tf_op jit(solution)/shard_map/ppermute | solution.py:12
  201.8 5.7 %collective-permute-start.8 = (bf16[1,1,48,384]{3,2,1,0:T(8,128)(2,1)S(1)}, bf16[1,1,48,384]{3,2,1,0:T(8,128)(2,1)S(1)}, u32[]{:S(2)}, u32[]{:S(2)}) collective-permute-start(bf16[1,1,48,384]{3,2,1,0:T(8,128)(2,1)S(1)} %get-tuple-element.145), channel_id=1, source_target_pairs={{0,1},{1,2},{2,3},{4,5},{5,6},{6,7},{8,9},{9,10},{10,11},{12,13},{... | collective-permute-start | bytes 110600 | tf_op jit(solution)/shard_map/ppermute | solution.py:20
  204.9 5.9 %collective-permute-start.9 = (bf16[1,1,48,384]{3,2,1,0:T(8,128)(2,1)S(1)}, bf16[1,1,48,384]{3,2,1,0:T(8,128)(2,1)S(1)}, u32[]{:S(2)}, u32[]{:S(2)}) collective-permute-start(bf16[1,1,48,384]{3,2,1,0:T(8,128)(2,1)S(1)} %get-tuple-element.146), channel_id=1, source_target_pairs={{1,0},{2,1},{3,2},{5,4},{6,5},{7,6},{9,8},{10,9},{11,10},{13,12},{... | collective-permute-start | bytes 110600 | tf_op jit(solution)/shard_map/ppermute | solution.py:23
  256.2 5.3 %collective-permute-start.10 = (bf16[1,1,96,384]{3,2,1,0:T(8,128)(2,1)S(1)}, bf16[1,1,96,384]{3,2,1,0:T(8,128)(2,1)S(1)}, u32[]{:S(2)}, u32[]{:S(2)}) collective-permute-start(bf16[1,1,96,384]{3,2,1,0:T(8,128)(2,1)S(1)} %get-tuple-element.137), channel_id=1, source_target_pairs={{0,1},{1,2},{2,3},{4,5},{5,6},{6,7},{8,9},{9,10},{10,11},{12,13},{... | collective-permute-start | bytes 221192 | tf_op jit(solution)/shard_map/ppermute | solution.py:20
  259.5 6.2 %collective-permute-start.11 = (bf16[1,1,96,384]{3,2,1,0:T(8,128)(2,1)S(1)}, bf16[1,1,96,384]{3,2,1,0:T(8,128)(2,1)S(1)}, u32[]{:S(2)}, u32[]{:S(2)}) collective-permute-start(bf16[1,1,96,384]{3,2,1,0:T(8,128)(2,1)S(1)} %get-tuple-element.138), channel_id=1, source_target_pairs={{1,0},{2,1},{3,2},{5,4},{6,5},{7,6},{9,8},{10,9},{11,10},{13,12},{... | collective-permute-start | bytes 221192 | tf_op jit(solution)/shard_map/ppermute | solution.py:23
  318.7 6.0 %collective-permute-start.12 = (bf16[1,1,192,384]{3,2,1,0:T(8,128)(2,1)S(1)}, bf16[1,1,192,384]{3,2,1,0:T(8,128)(2,1)S(1)}, u32[]{:S(2)}, u32[]{:S(2)}) collective-permute-start(bf16[1,1,192,384]{3,2,1,0:T(8,128)(2,1)S(1)} %get-tuple-element.131), channel_id=1, source_target_pairs={{0,1},{1,2},{2,3},{4,5},{5,6},{6,7},{8,9},{9,10},{10,11},{12,13},{... | collective-permute-start | bytes 442376 | tf_op jit(solution)/shard_map/ppermute | solution.py:20
  322.1 7.0 %collective-permute-start.13 = (bf16[1,1,192,384]{3,2,1,0:T(8,128)(2,1)S(1)}, bf16[1,1,192,384]{3,2,1,0:T(8,128)(2,1)S(1)}, u32[]{:S(2)}, u32[]{:S(2)}) collective-permute-start(bf16[1,1,192,384]{3,2,1,0:T(8,128)(2,1)S(1)} %get-tuple-element.132), channel_id=1, source_target_pairs={{1,0},{2,1},{3,2},{5,4},{6,5},{7,6},{9,8},{10,9},{11,10},{13,12},{... | collective-permute-start | bytes 442376 | tf_op jit(solution)/shard_map/ppermute | solution.py:23
  374.1 7.2 %collective-permute-start.14 = (bf16[1,1,192,384]{3,2,1,0:T(8,128)(2,1)S(1)}, bf16[1,1,192,384]{3,2,1,0:T(8,128)(2,1)S(1)}, u32[]{:S(2)}, u32[]{:S(2)}) collective-permute-start(bf16[1,1,192,384]{3,2,1,0:T(8,128)(2,1)S(1)} %slice.1044), channel_id=1, source_target_pairs={{1,0},{2,1},{3,2},{5,4},{6,5},{7,6},{9,8},{10,9},{11,10},{13,12},{... | collective-permute-start | bytes 442376 | tf_op jit(solution)/shard_map/ppermute | solution.py:12
  386.2 5.3 %collective-permute-start.15 = (bf16[1,1,96,384]{3,2,1,0:T(8,128)(2,1)S(1)}, bf16[1,1,96,384]{3,2,1,0:T(8,128)(2,1)S(1)}, u32[]{:S(2)}, u32[]{:S(2)}) collective-permute-start(bf16[1,1,96,384]{3,2,1,0:T(8,128)(2,1)S(1)} %get-tuple-element.135), channel_id=1, source_target_pairs={{0,1},{1,2},{2,3},{4,5},{5,6},{6,7},{8,9},{9,10},{10,11},{12,13},{... | collective-permute-start | bytes 221192 | tf_op jit(solution)/shard_map/ppermute | solution.py:20
  389.6 6.2 %collective-permute-start.16 = (bf16[1,1,96,384]{3,2,1,0:T(8,128)(2,1)S(1)}, bf16[1,1,96,384]{3,2,1,0:T(8,128)(2,1)S(1)}, u32[]{:S(2)}, u32[]{:S(2)}) collective-permute-start(bf16[1,1,96,384]{3,2,1,0:T(8,128)(2,1)S(1)} %get-tuple-element.136), channel_id=1, source_target_pairs={{1,0},{2,1},{3,2},{5,4},{6,5},{7,6},{9,8},{10,9},{11,10},{13,12},{... | collective-permute-start | bytes 221192 | tf_op jit(solution)/shard_map/ppermute | solution.py:23
  438.1 6.2 %collective-permute-start.17 = (bf16[1,1,96,384]{3,2,1,0:T(8,128)(2,1)S(1)}, bf16[1,1,96,384]{3,2,1,0:T(8,128)(2,1)S(1)}, u32[]{:S(2)}, u32[]{:S(2)}) collective-permute-start(bf16[1,1,96,384]{3,2,1,0:T(8,128)(2,1)S(1)} %slice.1062), channel_id=1, source_target_pairs={{1,0},{2,1},{3,2},{5,4},{6,5},{7,6},{9,8},{10,9},{11,10},{13,12},{... | collective-permute-start | bytes 221192 | tf_op jit(solution)/shard_map/ppermute | solution.py:12
  446.0 5.0 %collective-permute-start.18 = (bf16[1,1,48,384]{3,2,1,0:T(8,128)(2,1)S(1)}, bf16[1,1,48,384]{3,2,1,0:T(8,128)(2,1)S(1)}, u32[]{:S(2)}, u32[]{:S(2)}) collective-permute-start(bf16[1,1,48,384]{3,2,1,0:T(8,128)(2,1)S(1)} %get-tuple-element.143), channel_id=1, source_target_pairs={{0,1},{1,2},{2,3},{4,5},{5,6},{6,7},{8,9},{9,10},{10,11},{12,13},{... | collective-permute-start | bytes 110600 | tf_op jit(solution)/shard_map/ppermute | solution.py:20
  449.4 5.9 %collective-permute-start.19 = (bf16[1,1,48,384]{3,2,1,0:T(8,128)(2,1)S(1)}, bf16[1,1,48,384]{3,2,1,0:T(8,128)(2,1)S(1)}, u32[]{:S(2)}, u32[]{:S(2)}) collective-permute-start(bf16[1,1,48,384]{3,2,1,0:T(8,128)(2,1)S(1)} %get-tuple-element.144), channel_id=1, source_target_pairs={{1,0},{2,1},{3,2},{5,4},{6,5},{7,6},{9,8},{10,9},{11,10},{13,12},{... | collective-permute-start | bytes 110600 | tf_op jit(solution)/shard_map/ppermute | solution.py:23
  (54 other events, 1481.4 us)
where the time goes:
time: 499 us; the launch traced here: 496 us
  blocking collectives  318 us (64%)
  waiting for transfers between devices  49.7 us (10%)
  other arithmetic  43 us (9%)
  starting transfers between devices  42.1 us (8%)
  local copies, waits for them, and re-layouts  24.9 us (5%)
  matrix products  11.5 us (2%)
  between operations  6.92 us (1%)
    psum x8, blocking collectives, normalize(): lax.psum((jnp.sum(projected, axis=(0, 1, 2)), jnp.sum(projected * project...  318 us
    ppermute x8, waiting for transfers between devices, extended_2(): lax.ppermute(lax.slice_in_dim(block, 0, width, axis=dim), axis, backward)  31.3 us
    ppermute x8, starting transfers between devices, extended_2(): lax.ppermute(lax.slice_in_dim(block, block.shape[dim] - width, None, axis...  26.1 us
    convert_element_type x8, other arithmetic, weighted_join_activate(): return jax.nn.silu(running / weight_sum).astype(jnp.bfloat16)  16.5 us
    ppermute x4, waiting for transfers between devices, from_behind(): return lax.ppermute(block, axis, route)  15.3 us
    dot_general x8, matrix products, separable(): jnp.dot(spatial.reshape(-1, spatial.shape[-1]), projection, preferred_ele...  11.5 us
    ppermute x8, starting transfers between devices, extended_2(): lax.ppermute(lax.slice_in_dim(block, 0, width, axis=dim), axis, backward)  10.7 us
  transfers between devices with their start and end apart: 20, of which 18 were waited for; matrix products, arithmetic and copies ran while one was open for 1% of the time, Pallas kernels for 0%

commit v1 on v0

--- a/solution.py
+++ b/solution.py
@@ -74,8 +74,11 @@
         * lax.axis_size("rows")
     )
     totals, squares = lax.psum(
-        (jnp.sum(projected, axis=(0, 1, 2)), jnp.sum(projected * projected, axis=(0, 1, 2))),
-        ("batch", "rows"),
+        lax.psum(
+            (jnp.sum(projected, axis=(0, 1, 2)), jnp.sum(projected * projected, axis=(0, 1, 2))),
+            "rows",
+        ),
+        "batch",
     )
     center = totals / count
     spread = squares / count - center * center

time: 499 us -> 349 us (0.70)
  blocking collectives: 318 us -> 165 us
    psum x8, blocking collectives: 318 us -> 70.2 us  [normalize(): lax.psum((jnp.sum(projected, axis=(0, 1, 2)), jnp.sum(projected * project...]
    psum x0 -> x8, blocking collectives: none -> 94.4 us  [normalize(): lax.psum(lax.psum((jnp.sum(projected, axis=(0, 1, 2)), jnp.sum(projected...]
  transfers between devices with their start and end apart: 20 -> 20, of which waited for: 18 -> 18; matrix products, arithmetic and copies ran while one was open for 1% -> 2% of each run, Pallas kernels for 0% -> 0%
where the time goes in v1:
time: 349 us; the launch traced here: 347 us
  blocking collectives  165 us (47%)
  waiting for transfers between devices  51.3 us (15%)
  starting transfers between devices  45 us (13%)
  other arithmetic  43 us (12%)
  local copies, waits for them, and re-layouts  24.9 us (7%)
  matrix products  11.5 us (3%)
  between operations  6.89 us (2%)
    psum x8, blocking collectives, normalize(): lax.psum(lax.psum((jnp.sum(projected, axis=(0, 1, 2)), jnp.sum(projected...  94.4 us
    psum x8, blocking collectives, normalize(): lax.psum((jnp.sum(projected, axis=(0, 1, 2)), jnp.sum(projected * project...  70.2 us
    ppermute x8, waiting for transfers between devices, extended_2(): lax.ppermute(lax.slice_in_dim(block, 0, width, axis=dim), axis, backward)  30.8 us
    ppermute x8, starting transfers between devices, extended_2(): lax.ppermute(lax.slice_in_dim(block, block.shape[dim] - width, None, axis...  29.4 us
    convert_element_type x8, other arithmetic, weighted_join_activate(): return jax.nn.silu(running / weight_sum).astype(jnp.bfloat16)  16.5 us
    ppermute x4, waiting for transfers between devices, from_behind(): return lax.ppermute(block, axis, route)  16.3 us
    dot_general x8, matrix products, separable(): jnp.dot(spatial.reshape(-1, spatial.shape[-1]), projection, preferred_ele...  11.5 us
    ppermute x8, starting transfers between devices, extended_2(): lax.ppermute(lax.slice_in_dim(block, 0, width, axis=dim), axis, backward)  10.3 us
  transfers between devices with their start and end apart: 20, of which 18 were waited for; matrix products, arithmetic and copies ran while one was open for 2% of the time, Pallas kernels for 0%

profile of v1, /device:TPU:0, one launch (start us, length us, event | category | flops | bytes accessed | tf_op | source)
XLA Modules:
  0.0 347.3 jit_solution(6982909369972522581)
XLA Ops:
  7.4 5.0 %collective-permute-start = (bf16[1,1,96,384]{3,2,1,0:T(8,128)(2,1)S(1)}, bf16[1,1,96,384]{3,2,1,0:T(8,128)(2,1)S(1)}, u32[]{:S(2)}, u32[]{:S(2)}) collective-permute-start(bf16[1,1,96,384]{3,2,1,0:T(8,128)(2,1)S(1)} %get-tuple-element.157), channel_id=1, source_target_pairs={{0,1},{1,2},{2,3},{4,5},{5,6},{6,7},{8,9},{9,10},{10,11},{12,13},{... | collective-permute-start | bytes 221192 | tf_op jit(solution)/shard_map/ppermute | solution.py:20
  20.6 10.8 %all-reduce.23 = (f32[384]{0:T(512)S(1)}, f32[384]{0:T(512)S(1)}) all-reduce(f32[384]{0:T(512)S(1)} %get-tuple-element.14, f32[384]{0:T(512)S(1)} %get-tuple-element.13), channel_id=1, replica_groups=mesh['batch'=8,'rows'=4] {'rows'}, use_global_device_ids=true, to_apply=%region_5.6 | all-reduce | flops 768 | bytes 6144 | tf_op jit(solution)/shard_map/psum | solution.py:77
  31.4 11.8 %all-reduce.15 = (f32[384]{0:T(512)S(1)}, f32[384]{0:T(512)S(1)}) all-reduce(f32[384]{0:T(512)S(1)} %get-tuple-element.145, f32[384]{0:T(512)S(1)} %get-tuple-element.146), channel_id=1, replica_groups=mesh['batch'=8,'rows'=4] {'batch'}, use_global_device_ids=true, to_apply=%region_6.7 | all-reduce | flops 768 | bytes 6144 | tf_op jit(solution)/shard_map/psum | solution.py:76
  56.3 4.1 %collective-permute-done.3 = bf16[1,1,192,384]{3,2,1,0:T(8,128)(2,1)S(1)} collective-permute-done((bf16[1,1,192,384]{3,2,1,0:T(8,128)(2,1)S(1)}, bf16[1,1,192,384]{3,2,1,0:T(8,128)(2,1)S(1)}, u32[]{:S(2)}, u32[]{:S(2)}) %collective-permute-start.3) | collective-permute-done | bytes 147488 | tf_op jit(solution)/shard_map/ppermute | solution.py:23
  65.2 8.8 %all-reduce.22 = (f32[384]{0:T(512)S(1)}, f32[384]{0:T(512)S(1)}) all-reduce(f32[384]{0:T(512)S(1)} %get-tuple-element.6, f32[384]{0:T(512)S(1)} %get-tuple-element.5), channel_id=1, replica_groups=mesh['batch'=8,'rows'=4] {'rows'}, use_global_device_ids=true, to_apply=%region_12.13 | all-reduce | flops 768 | bytes 6144 | tf_op jit(solution)/shard_map/psum | solution.py:77
  74.0 11.8 %all-reduce.14 = (f32[384]{0:T(512)S(1)}, f32[384]{0:T(512)S(1)}) all-reduce(f32[384]{0:T(512)S(1)} %get-tuple-element.143, f32[384]{0:T(512)S(1)} %get-tuple-element.144), channel_id=1, replica_groups=mesh['batch'=8,'rows'=4] {'batch'}, use_global_device_ids=true, to_apply=%region_13.14 | all-reduce | flops 768 | bytes 6144 | tf_op jit(solution)/shard_map/psum | solution.py:76
  109.1 4.3 %collective-permute-done.6 = bf16[1,1,96,384]{3,2,1,0:T(8,128)(2,1)S(1)} collective-permute-done((bf16[1,1,96,384]{3,2,1,0:T(8,128)(2,1)S(1)}, bf16[1,1,96,384]{3,2,1,0:T(8,128)(2,1)S(1)}, u32[]{:S(2)}, u32[]{:S(2)}) %collective-permute-start.6) | collective-permute-done | bytes 73760 | tf_op jit(solution)/shard_map/ppermute | solution.py:23
  115.4 8.4 %all-reduce.21 = (f32[384]{0:T(512)S(1)}, f32[384]{0:T(512)S(1)}) all-reduce(f32[384]{0:T(512)S(1)} %get-tuple-element.12, f32[384]{0:T(512)S(1)} %get-tuple-element.11), channel_id=1, replica_groups=mesh['batch'=8,'rows'=4] {'rows'}, use_global_device_ids=true, to_apply=%region_20.21 | all-reduce | flops 768 | bytes 6144 | tf_op jit(solution)/shard_map/psum | solution.py:77
  123.8 12.0 %all-reduce.13 = (f32[384]{0:T(512)S(1)}, f32[384]{0:T(512)S(1)}) all-reduce(f32[384]{0:T(512)S(1)} %get-tuple-element.141, f32[384]{0:T(512)S(1)} %get-tuple-element.142), channel_id=1, replica_groups=mesh['batch'=8,'rows'=4] {'batch'}, use_global_device_ids=true, to_apply=%region_21.22 | all-reduce | flops 768 | bytes 6144 | tf_op jit(solution)/shard_map/psum | solution.py:76
  156.7 8.4 %all-reduce.20 = (f32[384]{0:T(512)S(1)}, f32[384]{0:T(512)S(1)}) all-reduce(f32[384]{0:T(512)S(1)} %get-tuple-element.18, f32[384]{0:T(512)S(1)} %get-tuple-element.17), channel_id=1, replica_groups=mesh['batch'=8,'rows'=4] {'rows'}, use_global_device_ids=true, to_apply=%region_28.29 | all-reduce | flops 768 | bytes 6144 | tf_op jit(solution)/shard_map/psum | solution.py:77
  165.1 11.8 %all-reduce.12 = (f32[384]{0:T(512)S(1)}, f32[384]{0:T(512)S(1)}) all-reduce(f32[384]{0:T(512)S(1)} %get-tuple-element.139, f32[384]{0:T(512)S(1)} %get-tuple-element.140), channel_id=1, replica_groups=mesh['batch'=8,'rows'=4] {'batch'}, use_global_device_ids=true, to_apply=%region_29.30 | all-reduce | flops 768 | bytes 6144 | tf_op jit(solution)/shard_map/psum | solution.py:76
  187.6 4.3 %collective-permute-done.11 = bf16[1,1,96,384]{3,2,1,0:T(8,128)(2,1)S(1)} collective-permute-done((bf16[1,1,96,384]{3,2,1,0:T(8,128)(2,1)S(1)}, bf16[1,1,96,384]{3,2,1,0:T(8,128)(2,1)S(1)}, u32[]{:S(2)}, u32[]{:S(2)}) %collective-permute-start.11) | collective-permute-done | bytes 73760 | tf_op jit(solution)/shard_map/ppermute | solution.py:23
  193.8 8.4 %all-reduce.19 = (f32[384]{0:T(512)S(1)}, f32[384]{0:T(512)S(1)}) all-reduce(f32[384]{0:T(512)S(1)} %get-tuple-element.10, f32[384]{0:T(512)S(1)} %get-tuple-element.9), channel_id=1, replica_groups=mesh['batch'=8,'rows'=4] {'rows'}, use_global_device_ids=true, to_apply=%region_35.36 | all-reduce | flops 768 | bytes 6144 | tf_op jit(solution)/shard_map/psum | solution.py:77
  202.2 11.8 %all-reduce.11 = (f32[384]{0:T(512)S(1)}, f32[384]{0:T(512)S(1)}) all-reduce(f32[384]{0:T(512)S(1)} %get-tuple-element.137, f32[384]{0:T(512)S(1)} %get-tuple-element.138), channel_id=1, replica_groups=mesh['batch'=8,'rows'=4] {'batch'}, use_global_device_ids=true, to_apply=%region_36.37 | all-reduce | flops 768 | bytes 6144 | tf_op jit(solution)/shard_map/psum | solution.py:76
  240.8 8.7 %all-reduce.18 = (f32[384]{0:T(512)S(1)}, f32[384]{0:T(512)S(1)}) all-reduce(f32[384]{0:T(512)S(1)} %get-tuple-element.4, f32[384]{0:T(512)S(1)} %get-tuple-element.3), channel_id=1, replica_groups=mesh['batch'=8,'rows'=4] {'rows'}, use_global_device_ids=true, to_apply=%region_42.43 | all-reduce | flops 768 | bytes 6144 | tf_op jit(solution)/shard_map/psum | solution.py:77
  249.5 11.8 %all-reduce.10 = (f32[384]{0:T(512)S(1)}, f32[384]{0:T(512)S(1)}) all-reduce(f32[384]{0:T(512)S(1)} %get-tuple-element.135, f32[384]{0:T(512)S(1)} %get-tuple-element.136), channel_id=1, replica_groups=mesh['batch'=8,'rows'=4] {'batch'}, use_global_device_ids=true, to_apply=%region_43.44 | all-reduce | flops 768 | bytes 6144 | tf_op jit(solution)/shard_map/psum | solution.py:76
  264.6 5.5 %collective-permute-done.14 = bf16[1,1,192,384]{3,2,1,0:T(8,128)(2,1)S(1)} collective-permute-done((bf16[1,1,192,384]{3,2,1,0:T(8,128)(2,1)S(1)}, bf16[1,1,192,384]{3,2,1,0:T(8,128)(2,1)S(1)}, u32[]{:S(2)}, u32[]{:S(2)}) %collective-permute-start.14) | collective-permute-done | bytes 147488 | tf_op jit(solution)/shard_map/ppermute | solution.py:12
  280.8 4.3 %collective-permute-done.16 = bf16[1,1,96,384]{3,2,1,0:T(8,128)(2,1)S(1)} collective-permute-done((bf16[1,1,96,384]{3,2,1,0:T(8,128)(2,1)S(1)}, bf16[1,1,96,384]{3,2,1,0:T(8,128)(2,1)S(1)}, u32[]{:S(2)}, u32[]{:S(2)}) %collective-permute-start.16) | collective-permute-done | bytes 73760 | tf_op jit(solution)/shard_map/ppermute | solution.py:23
  287.1 8.4 %all-reduce.17 = (f32[384]{0:T(512)S(1)}, f32[384]{0:T(512)S(1)}) all-reduce(f32[384]{0:T(512)S(1)} %get-tuple-element.8, f32[384]{0:T(512)S(1)} %get-tuple-element.7), channel_id=1, replica_groups=mesh['batch'=8,'rows'=4] {'rows'}, use_global_device_ids=true, to_apply=%region_50.51 | all-reduce | flops 768 | bytes 6144 | tf_op jit(solution)/shard_map/psum | solution.py:77
  295.5 11.8 %all-reduce.9 = (f32[384]{0:T(512)S(1)}, f32[384]{0:T(512)S(1)}) all-reduce(f32[384]{0:T(512)S(1)} %get-tuple-element.133, f32[384]{0:T(512)S(1)} %get-tuple-element.134), channel_id=1, replica_groups=mesh['batch'=8,'rows'=4] {'batch'}, use_global_device_ids=true, to_apply=%region_51.52 | all-reduce | flops 768 | bytes 6144 | tf_op jit(solution)/shard_map/psum | solution.py:76
  309.4 4.3 %collective-permute-done.17 = bf16[1,1,96,384]{3,2,1,0:T(8,128)(2,1)S(1)} collective-permute-done((bf16[1,1,96,384]{3,2,1,0:T(8,128)(2,1)S(1)}, bf16[1,1,96,384]{3,2,1,0:T(8,128)(2,1)S(1)}, u32[]{:S(2)}, u32[]{:S(2)}) %collective-permute-start.17) | collective-permute-done | bytes 73760 | tf_op jit(solution)/shard_map/ppermute | solution.py:12
  320.9 4.2 %collective-permute-done.19 = bf16[1,1,48,384]{3,2,1,0:T(8,128)(2,1)S(1)} collective-permute-done((bf16[1,1,48,384]{3,2,1,0:T(8,128)(2,1)S(1)}, bf16[1,1,48,384]{3,2,1,0:T(8,128)(2,1)S(1)}, u32[]{:S(2)}, u32[]{:S(2)}) %collective-permute-start.19) | collective-permute-done | bytes 36896 | tf_op jit(solution)/shard_map/ppermute | solution.py:23
  326.5 8.4 %all-reduce.16 = (f32[384]{0:T(512)S(1)}, f32[384]{0:T(512)S(1)}) all-reduce(f32[384]{0:T(512)S(1)} %get-tuple-element.16, f32[384]{0:T(512)S(1)} %get-tuple-element.15), channel_id=1, replica_groups=mesh['batch'=8,'rows'=4] {'rows'}, use_global_device_ids=true, to_apply=%region_58.59 | all-reduce | flops 768 | bytes 6144 | tf_op jit(solution)/shard_map/psum | solution.py:77
  334.9 11.8 %all-reduce.8 = (f32[384]{0:T(512)S(1)}, f32[384]{0:T(512)S(1)}) all-reduce(f32[384]{0:T(512)S(1)} %get-tuple-element.131, f32[384]{0:T(512)S(1)} %get-tuple-element.132), channel_id=1, replica_groups=mesh['batch'=8,'rows'=4] {'batch'}, use_global_device_ids=true, to_apply=%region_59.60 | all-reduce | flops 768 | bytes 6144 | tf_op jit(solution)/shard_map/psum | solution.py:76
  (251 shorter events, 139.9 us)
Async XLA Ops:
  7.4 9.0 %collective-permute-start = (bf16[1,1,96,384]{3,2,1,0:T(8,128)(2,1)S(1)}, bf16[1,1,96,384]{3,2,1,0:T(8,128)(2,1)S(1)}, u32[]{:S(2)}, u32[]{:S(2)}) collective-permute-start(bf16[1,1,96,384]{3,2,1,0:T(8,128)(2,1)S(1)} %get-tuple-element.157), channel_id=1, source_target_pairs={{0,1},{1,2},{2,3},{4,5},{5,6},{6,7},{8,9},{9,10},{10,11},{12,13},{... | collective-permute-start | bytes 221192 | tf_op jit(solution)/shard_map/ppermute | solution.py:20
  12.4 6.2 %collective-permute-start.1 = (bf16[1,1,96,384]{3,2,1,0:T(8,128)(2,1)S(1)}, bf16[1,1,96,384]{3,2,1,0:T(8,128)(2,1)S(1)}, u32[]{:S(2)}, u32[]{:S(2)}) collective-permute-start(bf16[1,1,96,384]{3,2,1,0:T(8,128)(2,1)S(1)} %get-tuple-element.158), channel_id=1, source_target_pairs={{1,0},{2,1},{3,2},{5,4},{6,5},{7,6},{9,8},{10,9},{11,10},{13,12},{... | collective-permute-start | bytes 221192 | tf_op jit(solution)/shard_map/ppermute | solution.py:23
  16.4 163.8 %copy-start.21 = (f32[384]{0:T(512)}, f32[384]{0:T(512)S(1)}, u32[]{:S(2)}) copy-start(f32[384]{0:T(512)S(1)} %get-tuple-element.31) | copy-start | bytes 4612
  51.6 4.7 %collective-permute-start.2 = (bf16[1,1,192,384]{3,2,1,0:T(8,128)(2,1)S(1)}, bf16[1,1,192,384]{3,2,1,0:T(8,128)(2,1)S(1)}, u32[]{:S(2)}, u32[]{:S(2)}) collective-permute-start(bf16[1,1,192,384]{3,2,1,0:T(8,128)(2,1)S(1)} %get-tuple-element.149), channel_id=1, source_target_pairs={{0,1},{1,2},{2,3},{4,5},{5,6},{6,7},{8,9},{9,10},{10,11},{12,13},{... | collective-permute-start | bytes 442376 | tf_op jit(solution)/shard_map/ppermute | solution.py:20
  53.2 7.2 %collective-permute-start.3 = (bf16[1,1,192,384]{3,2,1,0:T(8,128)(2,1)S(1)}, bf16[1,1,192,384]{3,2,1,0:T(8,128)(2,1)S(1)}, u32[]{:S(2)}, u32[]{:S(2)}) collective-permute-start(bf16[1,1,192,384]{3,2,1,0:T(8,128)(2,1)S(1)} %get-tuple-element.150), channel_id=1, source_target_pairs={{1,0},{2,1},{3,2},{5,4},{6,5},{7,6},{9,8},{10,9},{11,10},{13,12},{... | collective-permute-start | bytes 442376 | tf_op jit(solution)/shard_map/ppermute | solution.py:23
  88.1 7.8 %collective-permute-start.4 = (bf16[1,1,192,384]{3,2,1,0:T(8,128)(2,1)}, bf16[1,1,192,384]{3,2,1,0:T(8,128)(2,1)}, u32[]{:S(2)}, u32[]{:S(2)}) collective-permute-start(bf16[1,1,192,384]{3,2,1,0:T(8,128)(2,1)} %slice.974), channel_id=1, source_target_pairs={{1,0},{2,1},{3,2},{5,4},{6,5},{7,6},{9,8},{10,9},{11,10},{13,12},{... | collective-permute-start | bytes 442376 | tf_op jit(solution)/shard_map/ppermute | solution.py:12
  103.7 5.4 %collective-permute-start.5 = (bf16[1,1,96,384]{3,2,1,0:T(8,128)(2,1)S(1)}, bf16[1,1,96,384]{3,2,1,0:T(8,128)(2,1)S(1)}, u32[]{:S(2)}, u32[]{:S(2)}) collective-permute-start(bf16[1,1,96,384]{3,2,1,0:T(8,128)(2,1)S(1)} %get-tuple-element.155), channel_id=1, source_target_pairs={{0,1},{1,2},{2,3},{4,5},{5,6},{6,7},{8,9},{9,10},{10,11},{12,13},{... | collective-permute-start | bytes 221192 | tf_op jit(solution)/shard_map/ppermute | solution.py:20
  107.2 6.2 %collective-permute-start.6 = (bf16[1,1,96,384]{3,2,1,0:T(8,128)(2,1)S(1)}, bf16[1,1,96,384]{3,2,1,0:T(8,128)(2,1)S(1)}, u32[]{:S(2)}, u32[]{:S(2)}) collective-permute-start(bf16[1,1,96,384]{3,2,1,0:T(8,128)(2,1)S(1)} %get-tuple-element.156), channel_id=1, source_target_pairs={{1,0},{2,1},{3,2},{5,4},{6,5},{7,6},{9,8},{10,9},{11,10},{13,12},{... | collective-permute-start | bytes 221192 | tf_op jit(solution)/shard_map/ppermute | solution.py:23
  115.4 64.7 %copy-start.1 = (f32[384,384]{1,0:T(8,128)}, f32[384,384]{1,0:T(8,128)S(1)}, u32[]{:S(2)}) copy-start(f32[384,384]{1,0:T(8,128)S(1)} %get-tuple-element.207) | copy-start | bytes 1769476
  115.4 61.5 %copy-start.32 = (f32[384]{0:T(512)S(1)}, f32[384]{0:T(512)}, u32[]{:S(2)}) copy-start(f32[384]{0:T(512)} %get-tuple-element.30) | copy-start | bytes 4612
  115.4 61.5 %copy-start.34 = (f32[384]{0:T(512)S(1)}, f32[384]{0:T(512)}, u32[]{:S(2)}) copy-start(f32[384]{0:T(512)} %get-tuple-element.225) | copy-start | bytes 4612
  135.9 6.2 %collective-permute-start.7 = (bf16[1,1,96,384]{3,2,1,0:T(8,128)(2,1)S(1)}, bf16[1,1,96,384]{3,2,1,0:T(8,128)(2,1)S(1)}, u32[]{:S(2)}, u32[]{:S(2)}) collective-permute-start(bf16[1,1,96,384]{3,2,1,0:T(8,128)(2,1)S(1)} %slice.992), channel_id=1, source_target_pairs={{1,0},{2,1},{3,2},{5,4},{6,5},{7,6},{9,8},{10,9},{11,10},{13,12},{... | collective-permute-start | bytes 221192 | tf_op jit(solution)/shard_map/ppermute | solution.py:12
  145.6 6.5 %collective-permute-start.8 = (bf16[1,1,48,384]{3,2,1,0:T(8,128)(2,1)S(1)}, bf16[1,1,48,384]{3,2,1,0:T(8,128)(2,1)S(1)}, u32[]{:S(2)}, u32[]{:S(2)}) collective-permute-start(bf16[1,1,48,384]{3,2,1,0:T(8,128)(2,1)S(1)} %get-tuple-element.161), channel_id=1, source_target_pairs={{0,1},{1,2},{2,3},{4,5},{5,6},{6,7},{8,9},{9,10},{10,11},{12,13},{... | collective-permute-start | bytes 110600 | tf_op jit(solution)/shard_map/ppermute | solution.py:20
  149.4 5.9 %collective-permute-start.9 = (bf16[1,1,48,384]{3,2,1,0:T(8,128)(2,1)S(1)}, bf16[1,1,48,384]{3,2,1,0:T(8,128)(2,1)S(1)}, u32[]{:S(2)}, u32[]{:S(2)}) collective-permute-start(bf16[1,1,48,384]{3,2,1,0:T(8,128)(2,1)S(1)} %get-tuple-element.162), channel_id=1, source_target_pairs={{1,0},{2,1},{3,2},{5,4},{6,5},{7,6},{9,8},{10,9},{11,10},{13,12},{... | collective-permute-start | bytes 110600 | tf_op jit(solution)/shard_map/ppermute | solution.py:23
  181.8 5.8 %collective-permute-start.10 = (bf16[1,1,96,384]{3,2,1,0:T(8,128)(2,1)S(1)}, bf16[1,1,96,384]{3,2,1,0:T(8,128)(2,1)S(1)}, u32[]{:S(2)}, u32[]{:S(2)}) collective-permute-start(bf16[1,1,96,384]{3,2,1,0:T(8,128)(2,1)S(1)} %get-tuple-element.153), channel_id=1, source_target_pairs={{0,1},{1,2},{2,3},{4,5},{5,6},{6,7},{8,9},{9,10},{10,11},{12,13},{... | collective-permute-start | bytes 221192 | tf_op jit(solution)/shard_map/ppermute | solution.py:20
  185.6 6.2 %collective-permute-start.11 = (bf16[1,1,96,384]{3,2,1,0:T(8,128)(2,1)S(1)}, bf16[1,1,96,384]{3,2,1,0:T(8,128)(2,1)S(1)}, u32[]{:S(2)}, u32[]{:S(2)}) collective-permute-start(bf16[1,1,96,384]{3,2,1,0:T(8,128)(2,1)S(1)} %get-tuple-element.154), channel_id=1, source_target_pairs={{1,0},{2,1},{3,2},{5,4},{6,5},{7,6},{9,8},{10,9},{11,10},{13,12},{... | collective-permute-start | bytes 221192 | tf_op jit(solution)/shard_map/ppermute | solution.py:23
  225.0 7.0 %collective-permute-start.12 = (bf16[1,1,192,384]{3,2,1,0:T(8,128)(2,1)S(1)}, bf16[1,1,192,384]{3,2,1,0:T(8,128)(2,1)S(1)}, u32[]{:S(2)}, u32[]{:S(2)}) collective-permute-start(bf16[1,1,192,384]{3,2,1,0:T(8,128)(2,1)S(1)} %get-tuple-element.147), channel_id=1, source_target_pairs={{0,1},{1,2},{2,3},{4,5},{5,6},{6,7},{8,9},{9,10},{10,11},{12,13},{... | collective-permute-start | bytes 442376 | tf_op jit(solution)/shard_map/ppermute | solution.py:20
  228.9 7.2 %collective-permute-start.13 = (bf16[1,1,192,384]{3,2,1,0:T(8,128)(2,1)S(1)}, bf16[1,1,192,384]{3,2,1,0:T(8,128)(2,1)S(1)}, u32[]{:S(2)}, u32[]{:S(2)}) collective-permute-start(bf16[1,1,192,384]{3,2,1,0:T(8,128)(2,1)S(1)} %get-tuple-element.148), channel_id=1, source_target_pairs={{1,0},{2,1},{3,2},{5,4},{6,5},{7,6},{9,8},{10,9},{11,10},{13,12},{... | collective-permute-start | bytes 442376 | tf_op jit(solution)/shard_map/ppermute | solution.py:23
  262.5 7.6 %collective-permute-start.14 = (bf16[1,1,192,384]{3,2,1,0:T(8,128)(2,1)S(1)}, bf16[1,1,192,384]{3,2,1,0:T(8,128)(2,1)S(1)}, u32[]{:S(2)}, u32[]{:S(2)}) collective-permute-start(bf16[1,1,192,384]{3,2,1,0:T(8,128)(2,1)S(1)} %slice.1044), channel_id=1, source_target_pairs={{1,0},{2,1},{3,2},{5,4},{6,5},{7,6},{9,8},{10,9},{11,10},{13,12},{... | collective-permute-start | bytes 442376 | tf_op jit(solution)/shard_map/ppermute | solution.py:12
  275.0 5.8 %collective-permute-start.15 = (bf16[1,1,96,384]{3,2,1,0:T(8,128)(2,1)S(1)}, bf16[1,1,96,384]{3,2,1,0:T(8,128)(2,1)S(1)}, u32[]{:S(2)}, u32[]{:S(2)}) collective-permute-start(bf16[1,1,96,384]{3,2,1,0:T(8,128)(2,1)S(1)} %get-tuple-element.151), channel_id=1, source_target_pairs={{0,1},{1,2},{2,3},{4,5},{5,6},{6,7},{8,9},{9,10},{10,11},{12,13},{... | collective-permute-start | bytes 221192 | tf_op jit(solution)/shard_map/ppermute | solution.py:20
  278.9 6.2 %collective-permute-start.16 = (bf16[1,1,96,384]{3,2,1,0:T(8,128)(2,1)S(1)}, bf16[1,1,96,384]{3,2,1,0:T(8,128)(2,1)S(1)}, u32[]{:S(2)}, u32[]{:S(2)}) collective-permute-start(bf16[1,1,96,384]{3,2,1,0:T(8,128)(2,1)S(1)} %get-tuple-element.152), channel_id=1, source_target_pairs={{1,0},{2,1},{3,2},{5,4},{6,5},{7,6},{9,8},{10,9},{11,10},{13,12},{... | collective-permute-start | bytes 221192 | tf_op jit(solution)/shard_map/ppermute | solution.py:23
  307.5 6.2 %collective-permute-start.17 = (bf16[1,1,96,384]{3,2,1,0:T(8,128)(2,1)S(1)}, bf16[1,1,96,384]{3,2,1,0:T(8,128)(2,1)S(1)}, u32[]{:S(2)}, u32[]{:S(2)}) collective-permute-start(bf16[1,1,96,384]{3,2,1,0:T(8,128)(2,1)S(1)} %slice.1062), channel_id=1, source_target_pairs={{1,0},{2,1},{3,2},{5,4},{6,5},{7,6},{9,8},{10,9},{11,10},{13,12},{... | collective-permute-start | bytes 221192 | tf_op jit(solution)/shard_map/ppermute | solution.py:12
  315.4 5.5 %collective-permute-start.18 = (bf16[1,1,48,384]{3,2,1,0:T(8,128)(2,1)S(1)}, bf16[1,1,48,384]{3,2,1,0:T(8,128)(2,1)S(1)}, u32[]{:S(2)}, u32[]{:S(2)}) collective-permute-start(bf16[1,1,48,384]{3,2,1,0:T(8,128)(2,1)S(1)} %get-tuple-element.159), channel_id=1, source_target_pairs={{0,1},{1,2},{2,3},{4,5},{5,6},{6,7},{8,9},{9,10},{10,11},{12,13},{... | collective-permute-start | bytes 110600 | tf_op jit(solution)/shard_map/ppermute | solution.py:20
  319.2 5.9 %collective-permute-start.19 = (bf16[1,1,48,384]{3,2,1,0:T(8,128)(2,1)S(1)}, bf16[1,1,48,384]{3,2,1,0:T(8,128)(2,1)S(1)}, u32[]{:S(2)}, u32[]{:S(2)}) collective-permute-start(bf16[1,1,48,384]{3,2,1,0:T(8,128)(2,1)S(1)} %get-tuple-element.160), channel_id=1, source_target_pairs={{1,0},{2,1},{3,2},{5,4},{6,5},{7,6},{9,8},{10,9},{11,10},{13,12},{... | collective-permute-start | bytes 110600 | tf_op jit(solution)/shard_map/ppermute | solution.py:23
  (54 other events, 961.4 us)
